TPU v7x, 32 devices: a whole 2x2x4 slice. The times are simulated.
32 devices in a mesh: case: 2 (over y), blk: 4 (over z), freq: 4 (over x, core).
Axes of the slice: x: 2, y: 2, z: 4, core: 2. Of those that a mesh axis runs over, the one named last changes fastest.
Arguments:
- geometry: bfloat16 [3, 8192], P(None, ('case', 'blk')), parts along dimension 1, may hold values from -4 to 4
- modes: bfloat16 [4, 8192, 128], P('freq', ('case', 'blk')), parts along dimension 1, may hold values from -6 to 6
- reduced_freq: float32 [16], replicated, may hold values from 0.1 to 1.5
- freq_index: int32 [8, 3], P(('case', 'freq')), parts along dimension 0, may hold values from 0 to 15
Outputs:
- grad_geometry: float32 [3, 8192], P(None, ('case', 'blk', 'freq')), parts along dimension 1
- forces: float32 [8, 2, 32, 32], P(('case', 'freq')), parts along dimension 0
There are 2 independent parts, one for each index of `case`. A program takes and returns all parts, laid end to end along the dimension named above; an argument that names none is the same for every part. Nothing has to cross between parts.
All inputs are finite; a program needn't handle non-finite values.
Results may differ from a plain program's by a relative error of at most 0.003.
Values may be sent and summed in bfloat16 or wider, within the bound.
No kernel may reach another device: no remote copies, remote signals or barrier semaphores. Data moves between devices by JAX's collectives and lax.ppermute only.
A program may use at most 64 MiB of HBM per device.

v0:
```python
import math
import jax
import jax.numpy as jnp
from jax import lax
from jax.sharding import PartitionSpec as P

CHORD_SHIFT = 0.5
CORE_SQUARE = 0.25


def passed_along(value, axis, steps):
    count = lax.axis_size(axis)
    pairs = [(source, (source + steps) % count) for source in range(count)]
    return lax.ppermute(value, axis, pairs)


def prepare_sender(send_modes):
    columns = send_modes.shape[1] // 4
    flipped = jnp.concatenate([send_modes[:, 2 * columns :], send_modes[:, : 2 * columns]], axis=1)
    turned = jnp.concatenate(
        [
            send_modes[:, 3 * columns :],
            -send_modes[:, 2 * columns : 3 * columns],
            send_modes[:, columns : 2 * columns],
            -send_modes[:, :columns],
        ],
        axis=1,
    )
    paired = jnp.concatenate([flipped, turned], axis=0)
    strength = jnp.concatenate(
        [
            send_modes[:, 2 * columns :],
            jnp.concatenate(
                [-send_modes[:, 3 * columns :], send_modes[:, 2 * columns : 3 * columns]], axis=1
            ),
        ],
        axis=0,
    )
    return (paired, strength)


def block_terms(recv_geom, recv_modes, send_pos, paired, strength, wavenumber):
    send_count = send_pos.shape[1]
    coupled = lax.dot_general(
        recv_modes, paired, (((1,), (1,)), ((), ())), preferred_element_type=jnp.float32
    )
    real_part = coupled[:, :send_count]
    imag_part = coupled[:, send_count:]
    recv_pos = recv_geom.astype(jnp.float32)
    delta_x = recv_pos[0][:, None] + CHORD_SHIFT - send_pos[0][None, :]
    delta_y = recv_pos[1][:, None] - send_pos[1][None, :]
    delta_z = recv_pos[2][:, None] - send_pos[2][None, :]
    inverse = lax.rsqrt(delta_x * delta_x + delta_y * delta_y + delta_z * delta_z + CORE_SQUARE)
    phase = wavenumber * delta_x
    cosine = jnp.cos(phase)
    sine = jnp.sin(phase)
    along = cosine * real_part + sine * imag_part
    across = cosine * imag_part - sine * real_part
    cubed = inverse * inverse * inverse * along
    grad_x = wavenumber * inverse * across - delta_x * cubed
    grad_y = -delta_y * cubed
    grad_z = -delta_z * cubed
    row_grad = jnp.stack([grad_x.sum(axis=1), grad_y.sum(axis=1), grad_z.sum(axis=1)])
    col_grad = -jnp.stack([grad_x.sum(axis=0), grad_y.sum(axis=0), grad_z.sum(axis=0)])
    kernel = jnp.concatenate([cosine * inverse, -sine * inverse], axis=1).astype(jnp.bfloat16)
    pressure = jnp.dot(kernel, strength, preferred_element_type=jnp.float32)
    return (row_grad, col_grad, pressure)


def spread(stacked):
    return lax.psum_scatter(stacked, "freq", scatter_dimension=2, tiled=True)


def local(geometry, modes, reduced_freq, freq_index):
    row_count = geometry.shape[1]
    own_modes = modes[0]
    columns = own_modes.shape[1] // 4
    steps = freq_index.shape[1]
    table_size = reduced_freq.shape[0]
    selected = freq_index[0][:, None] == jnp.arange(table_size, dtype=jnp.int32)[None, :]
    wavenumbers = jnp.sum(jnp.where(selected, reduced_freq[None, :], 0.0), axis=1)
    local_block = (geometry, own_modes)
    sending = [local_block]
    current = local_block
    for offset in range(1, steps):
        current = passed_along((current[0], current[1]), "blk", 1)
        sending.append(current)
    block_rows = min(128, row_count)
    block_count = row_count // block_rows
    recv_geom = geometry.reshape(3, block_count, block_rows).transpose(1, 0, 2)
    recv_modes = own_modes.reshape(block_count, block_rows, 4 * columns)
    row_total = jnp.zeros((3, row_count), jnp.float32)
    pressure_total = jnp.zeros((row_count, 2 * columns), jnp.float32)
    col_parts = []
    for offset in range(steps):
        send_geom, send_modes = sending[offset]
        paired, strength = prepare_sender(send_modes)
        send_pos = send_geom.astype(jnp.float32)
        wavenumber = wavenumbers[offset]

        def visit(
            carry,
            operands,
            send_pos=send_pos,
            paired=paired,
            strength=strength,
            wavenumber=wavenumber,
        ):
            row_grad, col_grad, pressure = block_terms(
                operands[0], operands[1], send_pos, paired, strength, wavenumber
            )
            return (carry + col_grad, (row_grad, pressure))

        col_grad, (row_parts, pressure_parts) = lax.scan(
            visit, jnp.zeros((3, row_count), jnp.float32), (recv_geom, recv_modes)
        )
        row_total = row_total + row_parts.transpose(1, 0, 2).reshape(3, row_count)
        pressure_total = pressure_total + pressure_parts.reshape(row_count, 2 * columns)
        col_parts.append(col_grad)
    local_grad = row_total + col_parts[0]
    grad_scale = 1.0 / math.sqrt(columns * steps * row_count * lax.axis_size("freq"))
    total = local_grad
    for offset in range(1, steps):
        total = total + passed_along(col_parts[offset], "blk", -offset)
    result = spread((total * grad_scale)[None])[0]
    adjoint = own_modes[:, : 2 * columns].astype(jnp.float32)
    adj_real = adjoint[:, :columns]
    adj_imag = adjoint[:, columns:]
    press_real = pressure_total[:, :columns]
    press_imag = pressure_total[:, columns:]
    contract = (((0,), (0,)), ((), ()))
    force_real = lax.dot_general(
        adj_real, press_real, contract, precision=lax.Precision.HIGHEST
    ) + lax.dot_general(adj_imag, press_imag, contract, precision=lax.Precision.HIGHEST)
    force_imag = lax.dot_general(
        adj_real, press_imag, contract, precision=lax.Precision.HIGHEST
    ) - lax.dot_general(adj_imag, press_real, contract, precision=lax.Precision.HIGHEST)
    force_local = jnp.stack([force_real, force_imag])
    force_total = lax.psum(force_local, "blk")
    force_scale = 1.0 / math.sqrt(row_count * row_count * lax.axis_size("blk") * steps)
    return (result, (force_total * force_scale)[None])


def solution(mesh):
    return jax.shard_map(
        local,
        mesh=mesh,
        in_specs=(
            P(None, ("case", "blk")),
            P("freq", ("case", "blk"), None),
            P(),
            P(("case", "freq"), None),
        ),
        out_specs=(P(None, ("case", "blk", "freq")), P(("case", "freq"), None, None, None)),
        check_vma=False,
    )
```

profile of v0, /device:TPU:0, one launch (start us, length us, event | category | flops | bytes accessed | tf_op | source)
XLA Modules:
  0.0 178.1 jit_solution(9225079058068563746)
XLA Ops:
  7.2 3.1 %collective-permute-start.1 = (bf16[1024,128]{1,0:T(8,128)(2,1)}, bf16[1024,128]{1,0:T(8,128)(2,1)S(1)}, u32[]{:S(2)}, u32[]{:S(2)}) collective-permute-start(bf16[1024,128]{1,0:T(8,128)(2,1)} %bitcast.219), channel_id=1, source_target_pairs={{0,4},{4,8},{8,12},{12,0},{1,5},{5,9},{9,13},{13,1},{2,6},{6,10},{... | collective-permute-start | bytes 786440 | tf_op jit(solution)/shard_map/ppermute | solution.py:14
  16.0 3.0 %collective-permute-done = bf16[3,1024]{1,0:T(4,128)(2,1)S(1)} collective-permute-done((bf16[3,1024]{1,0:T(4,128)(2,1)}, bf16[3,1024]{1,0:T(4,128)(2,1)S(1)}, u32[]{:S(2)}, u32[]{:S(2)}) %collective-permute-start) | collective-permute-done | bytes 6176 | tf_op jit(solution)/shard_map/ppermute | solution.py:14
  19.0 34.4 %while.45 = (s32[]{:T(128)}, f32[3,1024]{1,0:T(4,128)S(1)}, f32[8,3,128]{2,1,0:T(4,128)S(1)}, f32[8,128,64]{1,2,0:T(8,128)S(1)}, f32[]{:T(128)}, /*index=5*/bf16...) while((s32[]{:T(128)}, f32[3,1024]{1,0:T(4,128)S(1)}, ...), condition=%wide.region_8.9_spmd.clone, body=%wide.region_1.8_spmd.clone.sunk | while | flops 106967936 | bytes 6464403 | solution.py:114
  19.4 3.2 %fusion.185 = (bf16[128,1024]{1,0:T(8,128)(2,1)S(1)}, bf16[128,1024]{1,0:T(8,128)(2,1)S(1)}, f32[128,1024]{1,0:T(8,128)S(1)}, f32[128,1024]{1,0:T(8,128)S(1)}) fusion(f32[1024]{0:T(1024)S(1)} %bitcast.228, f32[128]{0:T(128)S(1)} %get-tuple-element.645, f32[1024]{0:T(1024)S(1)} %bitcast.230, f32[128]{0:T(128)S(1)} %get-tuple-element.647, ...), kind=kLoop, calls=%fused_computation.25.clone.1 | loop fusion | flops 3670016 | bytes 2635268 | tf_op jit(solution)/shard_map/convert
  23.7 3.2 %fusion.185 = (bf16[128,1024]{1,0:T(8,128)(2,1)S(1)}, bf16[128,1024]{1,0:T(8,128)(2,1)S(1)}, f32[128,1024]{1,0:T(8,128)S(1)}, f32[128,1024]{1,0:T(8,128)S(1)}) fusion(f32[1024]{0:T(1024)S(1)} %bitcast.228, f32[128]{0:T(128)S(1)} %get-tuple-element.645, f32[1024]{0:T(1024)S(1)} %bitcast.230, f32[128]{0:T(128)S(1)} %get-tuple-element.647, ...), kind=kLoop, calls=%fused_computation.25.clone.1 | loop fusion | flops 3670016 | bytes 2635268 | tf_op jit(solution)/shard_map/convert
  28.0 3.2 %fusion.185 = (bf16[128,1024]{1,0:T(8,128)(2,1)S(1)}, bf16[128,1024]{1,0:T(8,128)(2,1)S(1)}, f32[128,1024]{1,0:T(8,128)S(1)}, f32[128,1024]{1,0:T(8,128)S(1)}) fusion(f32[1024]{0:T(1024)S(1)} %bitcast.228, f32[128]{0:T(128)S(1)} %get-tuple-element.645, f32[1024]{0:T(1024)S(1)} %bitcast.230, f32[128]{0:T(128)S(1)} %get-tuple-element.647, ...), kind=kLoop, calls=%fused_computation.25.clone.1 | loop fusion | flops 3670016 | bytes 2635268 | tf_op jit(solution)/shard_map/convert
  32.3 3.2 %fusion.185 = (bf16[128,1024]{1,0:T(8,128)(2,1)S(1)}, bf16[128,1024]{1,0:T(8,128)(2,1)S(1)}, f32[128,1024]{1,0:T(8,128)S(1)}, f32[128,1024]{1,0:T(8,128)S(1)}) fusion(f32[1024]{0:T(1024)S(1)} %bitcast.228, f32[128]{0:T(128)S(1)} %get-tuple-element.645, f32[1024]{0:T(1024)S(1)} %bitcast.230, f32[128]{0:T(128)S(1)} %get-tuple-element.647, ...), kind=kLoop, calls=%fused_computation.25.clone.1 | loop fusion | flops 3670016 | bytes 2635268 | tf_op jit(solution)/shard_map/convert
  36.6 3.2 %fusion.185 = (bf16[128,1024]{1,0:T(8,128)(2,1)S(1)}, bf16[128,1024]{1,0:T(8,128)(2,1)S(1)}, f32[128,1024]{1,0:T(8,128)S(1)}, f32[128,1024]{1,0:T(8,128)S(1)}) fusion(f32[1024]{0:T(1024)S(1)} %bitcast.228, f32[128]{0:T(128)S(1)} %get-tuple-element.645, f32[1024]{0:T(1024)S(1)} %bitcast.230, f32[128]{0:T(128)S(1)} %get-tuple-element.647, ...), kind=kLoop, calls=%fused_computation.25.clone.1 | loop fusion | flops 3670016 | bytes 2635268 | tf_op jit(solution)/shard_map/convert
  40.9 3.2 %fusion.185 = (bf16[128,1024]{1,0:T(8,128)(2,1)S(1)}, bf16[128,1024]{1,0:T(8,128)(2,1)S(1)}, f32[128,1024]{1,0:T(8,128)S(1)}, f32[128,1024]{1,0:T(8,128)S(1)}) fusion(f32[1024]{0:T(1024)S(1)} %bitcast.228, f32[128]{0:T(128)S(1)} %get-tuple-element.645, f32[1024]{0:T(1024)S(1)} %bitcast.230, f32[128]{0:T(128)S(1)} %get-tuple-element.647, ...), kind=kLoop, calls=%fused_computation.25.clone.1 | loop fusion | flops 3670016 | bytes 2635268 | tf_op jit(solution)/shard_map/convert
  45.2 3.2 %fusion.185 = (bf16[128,1024]{1,0:T(8,128)(2,1)S(1)}, bf16[128,1024]{1,0:T(8,128)(2,1)S(1)}, f32[128,1024]{1,0:T(8,128)S(1)}, f32[128,1024]{1,0:T(8,128)S(1)}) fusion(f32[1024]{0:T(1024)S(1)} %bitcast.228, f32[128]{0:T(128)S(1)} %get-tuple-element.645, f32[1024]{0:T(1024)S(1)} %bitcast.230, f32[128]{0:T(128)S(1)} %get-tuple-element.647, ...), kind=kLoop, calls=%fused_computation.25.clone.1 | loop fusion | flops 3670016 | bytes 2635268 | tf_op jit(solution)/shard_map/convert
  49.5 3.2 %fusion.185 = (bf16[128,1024]{1,0:T(8,128)(2,1)S(1)}, bf16[128,1024]{1,0:T(8,128)(2,1)S(1)}, f32[128,1024]{1,0:T(8,128)S(1)}, f32[128,1024]{1,0:T(8,128)S(1)}) fusion(f32[1024]{0:T(1024)S(1)} %bitcast.228, f32[128]{0:T(128)S(1)} %get-tuple-element.645, f32[1024]{0:T(1024)S(1)} %bitcast.230, f32[128]{0:T(128)S(1)} %get-tuple-element.647, ...), kind=kLoop, calls=%fused_computation.25.clone.1 | loop fusion | flops 3670016 | bytes 2635268 | tf_op jit(solution)/shard_map/convert
  56.0 34.7 %while.46 = (s32[]{:T(128)}, f32[3,1024]{1,0:T(4,128)S(1)}, f32[8,3,128]{2,1,0:T(4,128)S(1)}, f32[8,128,64]{1,2,0:T(8,128)S(1)}, f32[]{:T(128)}, /*index=5*/bf16...) while((s32[]{:T(128)}, f32[3,1024]{1,0:T(4,128)S(1)}, ...), condition=%wide.region_16.17_spmd.clone, body=%wide.region_9.16_spmd.clone.sunk | while | flops 106967936 | bytes 6464403 | solution.py:114
  56.4 3.2 %fusion.196 = (bf16[128,1024]{1,0:T(8,128)(2,1)S(1)}, bf16[128,1024]{1,0:T(8,128)(2,1)S(1)}, f32[128,1024]{1,0:T(8,128)S(1)}, f32[128,1024]{1,0:T(8,128)S(1)}) fusion(f32[1024]{0:T(1024)S(1)} %bitcast.232, f32[128]{0:T(128)S(1)} %get-tuple-element.671, f32[1024]{0:T(1024)S(1)} %bitcast.234, f32[128]{0:T(128)S(1)} %get-tuple-element.673, ...), kind=kLoop, calls=%fused_computation.77.clone.1 | loop fusion | flops 3670016 | bytes 2635268 | tf_op jit(solution)/shard_map/convert.2
  60.8 3.2 %fusion.196 = (bf16[128,1024]{1,0:T(8,128)(2,1)S(1)}, bf16[128,1024]{1,0:T(8,128)(2,1)S(1)}, f32[128,1024]{1,0:T(8,128)S(1)}, f32[128,1024]{1,0:T(8,128)S(1)}) fusion(f32[1024]{0:T(1024)S(1)} %bitcast.232, f32[128]{0:T(128)S(1)} %get-tuple-element.671, f32[1024]{0:T(1024)S(1)} %bitcast.234, f32[128]{0:T(128)S(1)} %get-tuple-element.673, ...), kind=kLoop, calls=%fused_computation.77.clone.1 | loop fusion | flops 3670016 | bytes 2635268 | tf_op jit(solution)/shard_map/convert.2
  65.1 3.2 %fusion.196 = (bf16[128,1024]{1,0:T(8,128)(2,1)S(1)}, bf16[128,1024]{1,0:T(8,128)(2,1)S(1)}, f32[128,1024]{1,0:T(8,128)S(1)}, f32[128,1024]{1,0:T(8,128)S(1)}) fusion(f32[1024]{0:T(1024)S(1)} %bitcast.232, f32[128]{0:T(128)S(1)} %get-tuple-element.671, f32[1024]{0:T(1024)S(1)} %bitcast.234, f32[128]{0:T(128)S(1)} %get-tuple-element.673, ...), kind=kLoop, calls=%fused_computation.77.clone.1 | loop fusion | flops 3670016 | bytes 2635268 | tf_op jit(solution)/shard_map/convert.2
  69.4 3.2 %fusion.196 = (bf16[128,1024]{1,0:T(8,128)(2,1)S(1)}, bf16[128,1024]{1,0:T(8,128)(2,1)S(1)}, f32[128,1024]{1,0:T(8,128)S(1)}, f32[128,1024]{1,0:T(8,128)S(1)}) fusion(f32[1024]{0:T(1024)S(1)} %bitcast.232, f32[128]{0:T(128)S(1)} %get-tuple-element.671, f32[1024]{0:T(1024)S(1)} %bitcast.234, f32[128]{0:T(128)S(1)} %get-tuple-element.673, ...), kind=kLoop, calls=%fused_computation.77.clone.1 | loop fusion | flops 3670016 | bytes 2635268 | tf_op jit(solution)/shard_map/convert.2
  73.8 3.2 %fusion.196 = (bf16[128,1024]{1,0:T(8,128)(2,1)S(1)}, bf16[128,1024]{1,0:T(8,128)(2,1)S(1)}, f32[128,1024]{1,0:T(8,128)S(1)}, f32[128,1024]{1,0:T(8,128)S(1)}) fusion(f32[1024]{0:T(1024)S(1)} %bitcast.232, f32[128]{0:T(128)S(1)} %get-tuple-element.671, f32[1024]{0:T(1024)S(1)} %bitcast.234, f32[128]{0:T(128)S(1)} %get-tuple-element.673, ...), kind=kLoop, calls=%fused_computation.77.clone.1 | loop fusion | flops 3670016 | bytes 2635268 | tf_op jit(solution)/shard_map/convert.2
  78.1 3.2 %fusion.196 = (bf16[128,1024]{1,0:T(8,128)(2,1)S(1)}, bf16[128,1024]{1,0:T(8,128)(2,1)S(1)}, f32[128,1024]{1,0:T(8,128)S(1)}, f32[128,1024]{1,0:T(8,128)S(1)}) fusion(f32[1024]{0:T(1024)S(1)} %bitcast.232, f32[128]{0:T(128)S(1)} %get-tuple-element.671, f32[1024]{0:T(1024)S(1)} %bitcast.234, f32[128]{0:T(128)S(1)} %get-tuple-element.673, ...), kind=kLoop, calls=%fused_computation.77.clone.1 | loop fusion | flops 3670016 | bytes 2635268 | tf_op jit(solution)/shard_map/convert.2
  82.5 3.2 %fusion.196 = (bf16[128,1024]{1,0:T(8,128)(2,1)S(1)}, bf16[128,1024]{1,0:T(8,128)(2,1)S(1)}, f32[128,1024]{1,0:T(8,128)S(1)}, f32[128,1024]{1,0:T(8,128)S(1)}) fusion(f32[1024]{0:T(1024)S(1)} %bitcast.232, f32[128]{0:T(128)S(1)} %get-tuple-element.671, f32[1024]{0:T(1024)S(1)} %bitcast.234, f32[128]{0:T(128)S(1)} %get-tuple-element.673, ...), kind=kLoop, calls=%fused_computation.77.clone.1 | loop fusion | flops 3670016 | bytes 2635268 | tf_op jit(solution)/shard_map/convert.2
  86.8 3.2 %fusion.196 = (bf16[128,1024]{1,0:T(8,128)(2,1)S(1)}, bf16[128,1024]{1,0:T(8,128)(2,1)S(1)}, f32[128,1024]{1,0:T(8,128)S(1)}, f32[128,1024]{1,0:T(8,128)S(1)}) fusion(f32[1024]{0:T(1024)S(1)} %bitcast.232, f32[128]{0:T(128)S(1)} %get-tuple-element.671, f32[1024]{0:T(1024)S(1)} %bitcast.234, f32[128]{0:T(128)S(1)} %get-tuple-element.673, ...), kind=kLoop, calls=%fused_computation.77.clone.1 | loop fusion | flops 3670016 | bytes 2635268 | tf_op jit(solution)/shard_map/convert.2
  90.8 2.6 %collective-permute-start.4 = (f32[3,1024]{1,0:T(4,128)S(1)}, f32[3,1024]{1,0:T(4,128)S(1)}, u32[]{:S(2)}, u32[]{:S(2)}) collective-permute-start(f32[3,1024]{1,0:T(4,128)S(1)} %get-tuple-element.168), channel_id=1, source_target_pairs={{0,12},{4,0},{8,4},{12,8},{1,13},{5,1},{9,5},{13,9},{2,14},{6,2},{... | collective-permute-start | bytes 36872 | tf_op jit(solution)/shard_map/ppermute | solution.py:14
  94.6 34.4 %while.47 = (s32[]{:T(128)}, f32[3,1024]{1,0:T(4,128)S(1)}, f32[8,3,128]{2,1,0:T(4,128)S(1)}, f32[8,128,64]{1,2,0:T(8,128)S(1)}, f32[]{:T(128)}, /*index=5*/bf16...) while((s32[]{:T(128)}, f32[3,1024]{1,0:T(4,128)S(1)}, ...), condition=%wide.region_24.25_spmd.clone, body=%wide.region_17.24_spmd.clone.sunk | while | flops 106967936 | bytes 6464403 | solution.py:114
  94.9 3.2 %fusion.207 = (bf16[128,1024]{1,0:T(8,128)(2,1)S(1)}, bf16[128,1024]{1,0:T(8,128)(2,1)S(1)}, f32[128,1024]{1,0:T(8,128)S(1)}, f32[128,1024]{1,0:T(8,128)S(1)}) fusion(f32[1024]{0:T(1024)S(1)} %bitcast.236, f32[128]{0:T(128)S(1)} %get-tuple-element.697, f32[1024]{0:T(1024)S(1)} %bitcast.238, f32[128]{0:T(128)S(1)} %get-tuple-element.699, ...), kind=kLoop, calls=%fused_computation.129.clone.1 | loop fusion | flops 3670016 | bytes 2635268 | tf_op jit(solution)/shard_map/convert.4
  99.2 3.2 %fusion.207 = (bf16[128,1024]{1,0:T(8,128)(2,1)S(1)}, bf16[128,1024]{1,0:T(8,128)(2,1)S(1)}, f32[128,1024]{1,0:T(8,128)S(1)}, f32[128,1024]{1,0:T(8,128)S(1)}) fusion(f32[1024]{0:T(1024)S(1)} %bitcast.236, f32[128]{0:T(128)S(1)} %get-tuple-element.697, f32[1024]{0:T(1024)S(1)} %bitcast.238, f32[128]{0:T(128)S(1)} %get-tuple-element.699, ...), kind=kLoop, calls=%fused_computation.129.clone.1 | loop fusion | flops 3670016 | bytes 2635268 | tf_op jit(solution)/shard_map/convert.4
  103.5 3.2 %fusion.207 = (bf16[128,1024]{1,0:T(8,128)(2,1)S(1)}, bf16[128,1024]{1,0:T(8,128)(2,1)S(1)}, f32[128,1024]{1,0:T(8,128)S(1)}, f32[128,1024]{1,0:T(8,128)S(1)}) fusion(f32[1024]{0:T(1024)S(1)} %bitcast.236, f32[128]{0:T(128)S(1)} %get-tuple-element.697, f32[1024]{0:T(1024)S(1)} %bitcast.238, f32[128]{0:T(128)S(1)} %get-tuple-element.699, ...), kind=kLoop, calls=%fused_computation.129.clone.1 | loop fusion | flops 3670016 | bytes 2635268 | tf_op jit(solution)/shard_map/convert.4
  107.8 3.2 %fusion.207 = (bf16[128,1024]{1,0:T(8,128)(2,1)S(1)}, bf16[128,1024]{1,0:T(8,128)(2,1)S(1)}, f32[128,1024]{1,0:T(8,128)S(1)}, f32[128,1024]{1,0:T(8,128)S(1)}) fusion(f32[1024]{0:T(1024)S(1)} %bitcast.236, f32[128]{0:T(128)S(1)} %get-tuple-element.697, f32[1024]{0:T(1024)S(1)} %bitcast.238, f32[128]{0:T(128)S(1)} %get-tuple-element.699, ...), kind=kLoop, calls=%fused_computation.129.clone.1 | loop fusion | flops 3670016 | bytes 2635268 | tf_op jit(solution)/shard_map/convert.4
  112.2 3.2 %fusion.207 = (bf16[128,1024]{1,0:T(8,128)(2,1)S(1)}, bf16[128,1024]{1,0:T(8,128)(2,1)S(1)}, f32[128,1024]{1,0:T(8,128)S(1)}, f32[128,1024]{1,0:T(8,128)S(1)}) fusion(f32[1024]{0:T(1024)S(1)} %bitcast.236, f32[128]{0:T(128)S(1)} %get-tuple-element.697, f32[1024]{0:T(1024)S(1)} %bitcast.238, f32[128]{0:T(128)S(1)} %get-tuple-element.699, ...), kind=kLoop, calls=%fused_computation.129.clone.1 | loop fusion | flops 3670016 | bytes 2635268 | tf_op jit(solution)/shard_map/convert.4
  116.5 3.2 %fusion.207 = (bf16[128,1024]{1,0:T(8,128)(2,1)S(1)}, bf16[128,1024]{1,0:T(8,128)(2,1)S(1)}, f32[128,1024]{1,0:T(8,128)S(1)}, f32[128,1024]{1,0:T(8,128)S(1)}) fusion(f32[1024]{0:T(1024)S(1)} %bitcast.236, f32[128]{0:T(128)S(1)} %get-tuple-element.697, f32[1024]{0:T(1024)S(1)} %bitcast.238, f32[128]{0:T(128)S(1)} %get-tuple-element.699, ...), kind=kLoop, calls=%fused_computation.129.clone.1 | loop fusion | flops 3670016 | bytes 2635268 | tf_op jit(solution)/shard_map/convert.4
  120.8 3.2 %fusion.207 = (bf16[128,1024]{1,0:T(8,128)(2,1)S(1)}, bf16[128,1024]{1,0:T(8,128)(2,1)S(1)}, f32[128,1024]{1,0:T(8,128)S(1)}, f32[128,1024]{1,0:T(8,128)S(1)}) fusion(f32[1024]{0:T(1024)S(1)} %bitcast.236, f32[128]{0:T(128)S(1)} %get-tuple-element.697, f32[1024]{0:T(1024)S(1)} %bitcast.238, f32[128]{0:T(128)S(1)} %get-tuple-element.699, ...), kind=kLoop, calls=%fused_computation.129.clone.1 | loop fusion | flops 3670016 | bytes 2635268 | tf_op jit(solution)/shard_map/convert.4
  125.1 3.2 %fusion.207 = (bf16[128,1024]{1,0:T(8,128)(2,1)S(1)}, bf16[128,1024]{1,0:T(8,128)(2,1)S(1)}, f32[128,1024]{1,0:T(8,128)S(1)}, f32[128,1024]{1,0:T(8,128)S(1)}) fusion(f32[1024]{0:T(1024)S(1)} %bitcast.236, f32[128]{0:T(128)S(1)} %get-tuple-element.697, f32[1024]{0:T(1024)S(1)} %bitcast.238, f32[128]{0:T(128)S(1)} %get-tuple-element.699, ...), kind=kLoop, calls=%fused_computation.129.clone.1 | loop fusion | flops 3670016 | bytes 2635268 | tf_op jit(solution)/shard_map/convert.4
  130.8 17.7 %psum.7 = f32[2,32,32]{1,2,0:T(8,128)S(1)} all-reduce(f32[2,32,32]{1,2,0:T(8,128)S(1)} %pad_maximum_fusion), channel_id=1, replica_groups=mesh['case'=2,'blk'=4,'freq'=4] {'blk'}, use_global_device_ids=true, to_apply=%region_26.27 | all-reduce | flops 2048 | bytes 16384 | tf_op jit(solution)/shard_map/psum | solution.py:139
  150.4 19.2 %reduce-scatter.4.cloned.1.call-done = f32[256,3]{1,0:T(8,128)} async-done(((f32[1024,3]{1,0:T(8,128)}), f32[256,3]{1,0:T(8,128)}) %reduce-scatter.4.cloned.1.call-update) | async-done | bytes 3088
  (248 shorter events, 40.4 us)
Async XLA Ops:
  7.2 162.5 %reduce-scatter.4.cloned.1.call-start = ((), (), s32[]{:S(2)}) async-start(), calls=%async_computation.1 | async-start | bytes 655360
  7.2 46.3 %collective-permute-start.1 = (bf16[1024,128]{1,0:T(8,128)(2,1)}, bf16[1024,128]{1,0:T(8,128)(2,1)S(1)}, u32[]{:S(2)}, u32[]{:S(2)}) collective-permute-start(bf16[1024,128]{1,0:T(8,128)(2,1)} %bitcast.219), channel_id=1, source_target_pairs={{0,4},{4,8},{8,12},{12,0},{1,5},{5,9},{9,13},{13,1},{2,6},{6,10},{... | collective-permute-start | bytes 786440 | tf_op jit(solution)/shard_map/ppermute | solution.py:14
  10.3 8.7 %collective-permute-start = (bf16[3,1024]{1,0:T(4,128)(2,1)}, bf16[3,1024]{1,0:T(4,128)(2,1)S(1)}, u32[]{:S(2)}, u32[]{:S(2)}) collective-permute-start(bf16[3,1024]{1,0:T(4,128)(2,1)} %param.10), channel_id=1, source_target_pairs={{0,4},{4,8},{8,12},{12,0},{1,5},{5,9},{9,13},{13,1},{2,6},{6,10},{... | collective-permute-start | bytes 18440 | tf_op jit(solution)/shard_map/ppermute | solution.py:14
  11.9 1.7 copy-start
  13.7 0.7 copy-start.2
  13.7 0.7 copy-start.3
  14.8 1.2 copy-start.1
  19.0 34.5 %collective-permute-start.2 = (bf16[3,1024]{1,0:T(4,128)(2,1)S(1)}, bf16[3,1024]{1,0:T(4,128)(2,1)S(1)}, u32[]{:S(2)}, u32[]{:S(2)}) collective-permute-start(bf16[3,1024]{1,0:T(4,128)(2,1)S(1)} %collective-permute-done), channel_id=1, source_target_pairs={{0,4},{4,8},{8,12},{12,0},{1,5},{5,9},{9,13},{13,1},{2,6},{6,10},{... | collective-permute-start | bytes 18440 | tf_op jit(solution)/shard_map/ppermute | solution.py:14
  54.7 38.7 %collective-permute-start.3 = (bf16[1024,128]{1,0:T(8,128)(2,1)S(1)}, bf16[1024,128]{1,0:T(8,128)(2,1)S(1)}, u32[]{:S(2)}, u32[]{:S(2)}) collective-permute-start(bf16[1024,128]{1,0:T(8,128)(2,1)S(1)} %collective-permute-done.1), channel_id=1, source_target_pairs={{0,4},{4,8},{8,12},{12,0},{1,5},{5,9},{9,13},{13,1},{2,6},{6,10},{... | collective-permute-start | bytes 786440 | tf_op jit(solution)/shard_map/ppermute | solution.py:14
  90.8 57.8 %collective-permute-start.4 = (f32[3,1024]{1,0:T(4,128)S(1)}, f32[3,1024]{1,0:T(4,128)S(1)}, u32[]{:S(2)}, u32[]{:S(2)}) collective-permute-start(f32[3,1024]{1,0:T(4,128)S(1)} %get-tuple-element.168), channel_id=1, source_target_pairs={{0,12},{4,0},{8,4},{12,8},{1,13},{5,1},{9,5},{13,9},{2,14},{6,2},{... | collective-permute-start | bytes 36872 | tf_op jit(solution)/shard_map/ppermute | solution.py:14
  130.2 18.4 %collective-permute-start.5 = (f32[3,1024]{1,0:T(4,128)S(1)}, f32[3,1024]{1,0:T(4,128)S(1)}, u32[]{:S(2)}, u32[]{:S(2)}) collective-permute-start(f32[3,1024]{1,0:T(4,128)S(1)} %get-tuple-element.169), channel_id=1, source_target_pairs={{0,8},{4,12},{8,0},{12,4},{1,9},{5,13},{9,1},{13,5},{2,10},{6,14},... | collective-permute-start | bytes 36872 | tf_op jit(solution)/shard_map/ppermute | solution.py:14
Sparse Core Ops, SparseCore 0:
  149.8 19.7 reduce-scatter.3
where the time goes:
time: 178 us
  other arithmetic  91.4 us (51%)
  waiting for transfers between devices  22.3 us (13%)
  blocking collectives  17.7 us (10%)
  matrix products  16.2 us (9%)
  between operations  14.3 us (8%)
  starting transfers between devices  9.26 us (5%)
  local copies, waits for them, and re-layouts  5.38 us (3%)
    another operation x24, other arithmetic  76.2 us
    unnamed x2, waiting for transfers between devices  19.3 us
    psum x1, blocking collectives, local(): force_total = lax.psum(force_local, 'blk')  17.7 us
    ppermute x6, starting transfers between devices, passed_along(): return lax.ppermute(value, axis, pairs)  9.23 us
    reduce_sum x24, other arithmetic, block_terms(): grad_y.sum(axis=1)  9.08 us
    dot_general x24, matrix products, block_terms(): pressure = jnp.dot(kernel, strength, preferred_element_type=jnp.float32)  7.89 us
    dot_general x24, matrix products, block_terms(): lax.dot_general(recv_modes, paired, (((1,), (1,)), ((), ())), preferred_e...  7.17 us
    unnamed x11, local copies, waits for them, and re-layouts  3.97 us
  transfers between devices with their start and end apart: 7, of which 2 were waited for; matrix products, arithmetic and copies ran while one was open for 61% of the time, Pallas kernels for 0%

commit v1 on v0

--- a/solution.py
+++ b/solution.py
@@ -136,7 +136,8 @@
         adj_real, press_imag, contract, precision=lax.Precision.HIGHEST
     ) - lax.dot_general(adj_imag, press_real, contract, precision=lax.Precision.HIGHEST)
     force_local = jnp.stack([force_real, force_imag])
-    force_total = lax.psum(force_local, "blk")
+    parts = lax.all_gather(force_local, "blk")
+    force_total = jnp.sum(parts, axis=0)
     force_scale = 1.0 / math.sqrt(row_count * row_count * lax.axis_size("blk") * steps)
     return (result, (force_total * force_scale)[None])
 

time: 178 us -> 176 us (0.989)
  blocking collectives: 17.7 us -> 13.6 us
    psum x1 -> x0, blocking collectives: 17.7 us -> none  [local(): force_total = lax.psum(force_local, 'blk')]
    all_gather x0 -> x1, blocking collectives: none -> 13.6 us  [local(): parts = lax.all_gather(force_local, 'blk')]
    unnamed x11 -> x12, local copies, waits for them, and re-layouts: 3.97 us -> 4.04 us
  transfers between devices with their start and end apart: 7 -> 7, of which waited for: 2 -> 2; matrix products, arithmetic and copies ran while one was open for 61% -> 62% of each run, Pallas kernels for 0% -> 0%
where the time goes in v1:
time: 176 us; the launch traced here: 175 us
  other arithmetic  91.5 us (52%)
  waiting for transfers between devices  23.7 us (13%)
  matrix products  16.2 us (9%)
  between operations  14.3 us (8%)
  blocking collectives  13.6 us (8%)
  starting transfers between devices  9.21 us (5%)
  local copies, waits for them, and re-layouts  5.53 us (3%)
    another operation x24, other arithmetic  76.2 us
    unnamed x2, waiting for transfers between devices  20.6 us
    all_gather x1, blocking collectives, local(): parts = lax.all_gather(force_local, 'blk')  13.6 us
    ppermute x6, starting transfers between devices, passed_along(): return lax.ppermute(value, axis, pairs)  9.17 us
    reduce_sum x24, other arithmetic, block_terms(): grad_y.sum(axis=1)  9.08 us
    dot_general x24, matrix products, block_terms(): pressure = jnp.dot(kernel, strength, preferred_element_type=jnp.float32)  7.89 us
    dot_general x24, matrix products, block_terms(): lax.dot_general(recv_modes, paired, (((1,), (1,)), ((), ())), preferred_e...  7.17 us
    unnamed x12, local copies, waits for them, and re-layouts  4.04 us
  transfers between devices with their start and end apart: 7, of which 2 were waited for; matrix products, arithmetic and copies ran while one was open for 62% of the time, Pallas kernels for 0%

profile of v1, /device:TPU:0, one launch (start us, length us, event | category | flops | bytes accessed | tf_op | source)
XLA Modules:
  0.0 175.4 jit_solution(17995739353087892729)
XLA Ops:
  7.2 3.1 %collective-permute-start.1 = (bf16[1024,128]{1,0:T(8,128)(2,1)}, bf16[1024,128]{1,0:T(8,128)(2,1)S(1)}, u32[]{:S(2)}, u32[]{:S(2)}) collective-permute-start(bf16[1024,128]{1,0:T(8,128)(2,1)} %bitcast.220), channel_id=1, source_target_pairs={{0,4},{4,8},{8,12},{12,0},{1,5},{5,9},{9,13},{13,1},{2,6},{6,10},{... | collective-permute-start | bytes 786440 | tf_op jit(solution)/shard_map/ppermute | solution.py:14
  16.0 3.0 %collective-permute-done = bf16[3,1024]{1,0:T(4,128)(2,1)S(1)} collective-permute-done((bf16[3,1024]{1,0:T(4,128)(2,1)}, bf16[3,1024]{1,0:T(4,128)(2,1)S(1)}, u32[]{:S(2)}, u32[]{:S(2)}) %collective-permute-start) | collective-permute-done | bytes 6176 | tf_op jit(solution)/shard_map/ppermute | solution.py:14
  19.0 34.4 %while.45 = (s32[]{:T(128)}, f32[3,1024]{1,0:T(4,128)S(1)}, f32[8,3,128]{2,1,0:T(4,128)S(1)}, f32[8,128,64]{1,2,0:T(8,128)S(1)}, f32[]{:T(128)}, /*index=5*/bf16...) while((s32[]{:T(128)}, f32[3,1024]{1,0:T(4,128)S(1)}, ...), condition=%wide.region_8.9_spmd.clone, body=%wide.region_1.8_spmd.clone.sunk | while | flops 106967936 | bytes 6464403 | solution.py:114
  19.4 3.2 %fusion.185 = (bf16[128,1024]{1,0:T(8,128)(2,1)S(1)}, bf16[128,1024]{1,0:T(8,128)(2,1)S(1)}, f32[128,1024]{1,0:T(8,128)S(1)}, f32[128,1024]{1,0:T(8,128)S(1)}) fusion(f32[1024]{0:T(1024)S(1)} %bitcast.229, f32[128]{0:T(128)S(1)} %get-tuple-element.641, f32[1024]{0:T(1024)S(1)} %bitcast.231, f32[128]{0:T(128)S(1)} %get-tuple-element.643, ...), kind=kLoop, calls=%fused_computation.25.clone.1 | loop fusion | flops 3670016 | bytes 2635268 | tf_op jit(solution)/shard_map/convert
  23.7 3.2 %fusion.185 = (bf16[128,1024]{1,0:T(8,128)(2,1)S(1)}, bf16[128,1024]{1,0:T(8,128)(2,1)S(1)}, f32[128,1024]{1,0:T(8,128)S(1)}, f32[128,1024]{1,0:T(8,128)S(1)}) fusion(f32[1024]{0:T(1024)S(1)} %bitcast.229, f32[128]{0:T(128)S(1)} %get-tuple-element.641, f32[1024]{0:T(1024)S(1)} %bitcast.231, f32[128]{0:T(128)S(1)} %get-tuple-element.643, ...), kind=kLoop, calls=%fused_computation.25.clone.1 | loop fusion | flops 3670016 | bytes 2635268 | tf_op jit(solution)/shard_map/convert
  28.0 3.2 %fusion.185 = (bf16[128,1024]{1,0:T(8,128)(2,1)S(1)}, bf16[128,1024]{1,0:T(8,128)(2,1)S(1)}, f32[128,1024]{1,0:T(8,128)S(1)}, f32[128,1024]{1,0:T(8,128)S(1)}) fusion(f32[1024]{0:T(1024)S(1)} %bitcast.229, f32[128]{0:T(128)S(1)} %get-tuple-element.641, f32[1024]{0:T(1024)S(1)} %bitcast.231, f32[128]{0:T(128)S(1)} %get-tuple-element.643, ...), kind=kLoop, calls=%fused_computation.25.clone.1 | loop fusion | flops 3670016 | bytes 2635268 | tf_op jit(solution)/shard_map/convert
  32.3 3.2 %fusion.185 = (bf16[128,1024]{1,0:T(8,128)(2,1)S(1)}, bf16[128,1024]{1,0:T(8,128)(2,1)S(1)}, f32[128,1024]{1,0:T(8,128)S(1)}, f32[128,1024]{1,0:T(8,128)S(1)}) fusion(f32[1024]{0:T(1024)S(1)} %bitcast.229, f32[128]{0:T(128)S(1)} %get-tuple-element.641, f32[1024]{0:T(1024)S(1)} %bitcast.231, f32[128]{0:T(128)S(1)} %get-tuple-element.643, ...), kind=kLoop, calls=%fused_computation.25.clone.1 | loop fusion | flops 3670016 | bytes 2635268 | tf_op jit(solution)/shard_map/convert
  36.6 3.2 %fusion.185 = (bf16[128,1024]{1,0:T(8,128)(2,1)S(1)}, bf16[128,1024]{1,0:T(8,128)(2,1)S(1)}, f32[128,1024]{1,0:T(8,128)S(1)}, f32[128,1024]{1,0:T(8,128)S(1)}) fusion(f32[1024]{0:T(1024)S(1)} %bitcast.229, f32[128]{0:T(128)S(1)} %get-tuple-element.641, f32[1024]{0:T(1024)S(1)} %bitcast.231, f32[128]{0:T(128)S(1)} %get-tuple-element.643, ...), kind=kLoop, calls=%fused_computation.25.clone.1 | loop fusion | flops 3670016 | bytes 2635268 | tf_op jit(solution)/shard_map/convert
  40.9 3.2 %fusion.185 = (bf16[128,1024]{1,0:T(8,128)(2,1)S(1)}, bf16[128,1024]{1,0:T(8,128)(2,1)S(1)}, f32[128,1024]{1,0:T(8,128)S(1)}, f32[128,1024]{1,0:T(8,128)S(1)}) fusion(f32[1024]{0:T(1024)S(1)} %bitcast.229, f32[128]{0:T(128)S(1)} %get-tuple-element.641, f32[1024]{0:T(1024)S(1)} %bitcast.231, f32[128]{0:T(128)S(1)} %get-tuple-element.643, ...), kind=kLoop, calls=%fused_computation.25.clone.1 | loop fusion | flops 3670016 | bytes 2635268 | tf_op jit(solution)/shard_map/convert
  45.2 3.2 %fusion.185 = (bf16[128,1024]{1,0:T(8,128)(2,1)S(1)}, bf16[128,1024]{1,0:T(8,128)(2,1)S(1)}, f32[128,1024]{1,0:T(8,128)S(1)}, f32[128,1024]{1,0:T(8,128)S(1)}) fusion(f32[1024]{0:T(1024)S(1)} %bitcast.229, f32[128]{0:T(128)S(1)} %get-tuple-element.641, f32[1024]{0:T(1024)S(1)} %bitcast.231, f32[128]{0:T(128)S(1)} %get-tuple-element.643, ...), kind=kLoop, calls=%fused_computation.25.clone.1 | loop fusion | flops 3670016 | bytes 2635268 | tf_op jit(solution)/shard_map/convert
  49.5 3.2 %fusion.185 = (bf16[128,1024]{1,0:T(8,128)(2,1)S(1)}, bf16[128,1024]{1,0:T(8,128)(2,1)S(1)}, f32[128,1024]{1,0:T(8,128)S(1)}, f32[128,1024]{1,0:T(8,128)S(1)}) fusion(f32[1024]{0:T(1024)S(1)} %bitcast.229, f32[128]{0:T(128)S(1)} %get-tuple-element.641, f32[1024]{0:T(1024)S(1)} %bitcast.231, f32[128]{0:T(128)S(1)} %get-tuple-element.643, ...), kind=kLoop, calls=%fused_computation.25.clone.1 | loop fusion | flops 3670016 | bytes 2635268 | tf_op jit(solution)/shard_map/convert
  56.0 34.7 %while.46 = (s32[]{:T(128)}, f32[3,1024]{1,0:T(4,128)S(1)}, f32[8,3,128]{2,1,0:T(4,128)S(1)}, f32[8,128,64]{1,2,0:T(8,128)S(1)}, f32[]{:T(128)}, /*index=5*/bf16...) while((s32[]{:T(128)}, f32[3,1024]{1,0:T(4,128)S(1)}, ...), condition=%wide.region_16.17_spmd.clone, body=%wide.region_9.16_spmd.clone.sunk | while | flops 106967936 | bytes 6464403 | solution.py:114
  56.4 3.2 %fusion.196 = (bf16[128,1024]{1,0:T(8,128)(2,1)S(1)}, bf16[128,1024]{1,0:T(8,128)(2,1)S(1)}, f32[128,1024]{1,0:T(8,128)S(1)}, f32[128,1024]{1,0:T(8,128)S(1)}) fusion(f32[1024]{0:T(1024)S(1)} %bitcast.233, f32[128]{0:T(128)S(1)} %get-tuple-element.667, f32[1024]{0:T(1024)S(1)} %bitcast.235, f32[128]{0:T(128)S(1)} %get-tuple-element.669, ...), kind=kLoop, calls=%fused_computation.77.clone.1 | loop fusion | flops 3670016 | bytes 2635268 | tf_op jit(solution)/shard_map/convert.2
  60.8 3.2 %fusion.196 = (bf16[128,1024]{1,0:T(8,128)(2,1)S(1)}, bf16[128,1024]{1,0:T(8,128)(2,1)S(1)}, f32[128,1024]{1,0:T(8,128)S(1)}, f32[128,1024]{1,0:T(8,128)S(1)}) fusion(f32[1024]{0:T(1024)S(1)} %bitcast.233, f32[128]{0:T(128)S(1)} %get-tuple-element.667, f32[1024]{0:T(1024)S(1)} %bitcast.235, f32[128]{0:T(128)S(1)} %get-tuple-element.669, ...), kind=kLoop, calls=%fused_computation.77.clone.1 | loop fusion | flops 3670016 | bytes 2635268 | tf_op jit(solution)/shard_map/convert.2
  65.1 3.2 %fusion.196 = (bf16[128,1024]{1,0:T(8,128)(2,1)S(1)}, bf16[128,1024]{1,0:T(8,128)(2,1)S(1)}, f32[128,1024]{1,0:T(8,128)S(1)}, f32[128,1024]{1,0:T(8,128)S(1)}) fusion(f32[1024]{0:T(1024)S(1)} %bitcast.233, f32[128]{0:T(128)S(1)} %get-tuple-element.667, f32[1024]{0:T(1024)S(1)} %bitcast.235, f32[128]{0:T(128)S(1)} %get-tuple-element.669, ...), kind=kLoop, calls=%fused_computation.77.clone.1 | loop fusion | flops 3670016 | bytes 2635268 | tf_op jit(solution)/shard_map/convert.2
  69.4 3.2 %fusion.196 = (bf16[128,1024]{1,0:T(8,128)(2,1)S(1)}, bf16[128,1024]{1,0:T(8,128)(2,1)S(1)}, f32[128,1024]{1,0:T(8,128)S(1)}, f32[128,1024]{1,0:T(8,128)S(1)}) fusion(f32[1024]{0:T(1024)S(1)} %bitcast.233, f32[128]{0:T(128)S(1)} %get-tuple-element.667, f32[1024]{0:T(1024)S(1)} %bitcast.235, f32[128]{0:T(128)S(1)} %get-tuple-element.669, ...), kind=kLoop, calls=%fused_computation.77.clone.1 | loop fusion | flops 3670016 | bytes 2635268 | tf_op jit(solution)/shard_map/convert.2
  73.8 3.2 %fusion.196 = (bf16[128,1024]{1,0:T(8,128)(2,1)S(1)}, bf16[128,1024]{1,0:T(8,128)(2,1)S(1)}, f32[128,1024]{1,0:T(8,128)S(1)}, f32[128,1024]{1,0:T(8,128)S(1)}) fusion(f32[1024]{0:T(1024)S(1)} %bitcast.233, f32[128]{0:T(128)S(1)} %get-tuple-element.667, f32[1024]{0:T(1024)S(1)} %bitcast.235, f32[128]{0:T(128)S(1)} %get-tuple-element.669, ...), kind=kLoop, calls=%fused_computation.77.clone.1 | loop fusion | flops 3670016 | bytes 2635268 | tf_op jit(solution)/shard_map/convert.2
  78.1 3.2 %fusion.196 = (bf16[128,1024]{1,0:T(8,128)(2,1)S(1)}, bf16[128,1024]{1,0:T(8,128)(2,1)S(1)}, f32[128,1024]{1,0:T(8,128)S(1)}, f32[128,1024]{1,0:T(8,128)S(1)}) fusion(f32[1024]{0:T(1024)S(1)} %bitcast.233, f32[128]{0:T(128)S(1)} %get-tuple-element.667, f32[1024]{0:T(1024)S(1)} %bitcast.235, f32[128]{0:T(128)S(1)} %get-tuple-element.669, ...), kind=kLoop, calls=%fused_computation.77.clone.1 | loop fusion | flops 3670016 | bytes 2635268 | tf_op jit(solution)/shard_map/convert.2
  82.5 3.2 %fusion.196 = (bf16[128,1024]{1,0:T(8,128)(2,1)S(1)}, bf16[128,1024]{1,0:T(8,128)(2,1)S(1)}, f32[128,1024]{1,0:T(8,128)S(1)}, f32[128,1024]{1,0:T(8,128)S(1)}) fusion(f32[1024]{0:T(1024)S(1)} %bitcast.233, f32[128]{0:T(128)S(1)} %get-tuple-element.667, f32[1024]{0:T(1024)S(1)} %bitcast.235, f32[128]{0:T(128)S(1)} %get-tuple-element.669, ...), kind=kLoop, calls=%fused_computation.77.clone.1 | loop fusion | flops 3670016 | bytes 2635268 | tf_op jit(solution)/shard_map/convert.2
  86.8 3.2 %fusion.196 = (bf16[128,1024]{1,0:T(8,128)(2,1)S(1)}, bf16[128,1024]{1,0:T(8,128)(2,1)S(1)}, f32[128,1024]{1,0:T(8,128)S(1)}, f32[128,1024]{1,0:T(8,128)S(1)}) fusion(f32[1024]{0:T(1024)S(1)} %bitcast.233, f32[128]{0:T(128)S(1)} %get-tuple-element.667, f32[1024]{0:T(1024)S(1)} %bitcast.235, f32[128]{0:T(128)S(1)} %get-tuple-element.669, ...), kind=kLoop, calls=%fused_computation.77.clone.1 | loop fusion | flops 3670016 | bytes 2635268 | tf_op jit(solution)/shard_map/convert.2
  90.8 2.6 %collective-permute-start.4 = (f32[3,1024]{1,0:T(4,128)S(1)}, f32[3,1024]{1,0:T(4,128)S(1)}, u32[]{:S(2)}, u32[]{:S(2)}) collective-permute-start(f32[3,1024]{1,0:T(4,128)S(1)} %get-tuple-element.168), channel_id=1, source_target_pairs={{0,12},{4,0},{8,4},{12,8},{1,13},{5,1},{9,5},{13,9},{2,14},{6,2},{... | collective-permute-start | bytes 36872 | tf_op jit(solution)/shard_map/ppermute | solution.py:14
  94.6 34.4 %while.47 = (s32[]{:T(128)}, f32[3,1024]{1,0:T(4,128)S(1)}, f32[8,3,128]{2,1,0:T(4,128)S(1)}, f32[8,128,64]{1,2,0:T(8,128)S(1)}, f32[]{:T(128)}, /*index=5*/bf16...) while((s32[]{:T(128)}, f32[3,1024]{1,0:T(4,128)S(1)}, ...), condition=%wide.region_24.25_spmd.clone, body=%wide.region_17.24_spmd.clone.sunk | while | flops 106967936 | bytes 6464403 | solution.py:114
  94.9 3.2 %fusion.207 = (bf16[128,1024]{1,0:T(8,128)(2,1)S(1)}, bf16[128,1024]{1,0:T(8,128)(2,1)S(1)}, f32[128,1024]{1,0:T(8,128)S(1)}, f32[128,1024]{1,0:T(8,128)S(1)}) fusion(f32[1024]{0:T(1024)S(1)} %bitcast.237, f32[128]{0:T(128)S(1)} %get-tuple-element.693, f32[1024]{0:T(1024)S(1)} %bitcast.239, f32[128]{0:T(128)S(1)} %get-tuple-element.695, ...), kind=kLoop, calls=%fused_computation.129.clone.1 | loop fusion | flops 3670016 | bytes 2635268 | tf_op jit(solution)/shard_map/convert.4
  99.2 3.2 %fusion.207 = (bf16[128,1024]{1,0:T(8,128)(2,1)S(1)}, bf16[128,1024]{1,0:T(8,128)(2,1)S(1)}, f32[128,1024]{1,0:T(8,128)S(1)}, f32[128,1024]{1,0:T(8,128)S(1)}) fusion(f32[1024]{0:T(1024)S(1)} %bitcast.237, f32[128]{0:T(128)S(1)} %get-tuple-element.693, f32[1024]{0:T(1024)S(1)} %bitcast.239, f32[128]{0:T(128)S(1)} %get-tuple-element.695, ...), kind=kLoop, calls=%fused_computation.129.clone.1 | loop fusion | flops 3670016 | bytes 2635268 | tf_op jit(solution)/shard_map/convert.4
  103.5 3.2 %fusion.207 = (bf16[128,1024]{1,0:T(8,128)(2,1)S(1)}, bf16[128,1024]{1,0:T(8,128)(2,1)S(1)}, f32[128,1024]{1,0:T(8,128)S(1)}, f32[128,1024]{1,0:T(8,128)S(1)}) fusion(f32[1024]{0:T(1024)S(1)} %bitcast.237, f32[128]{0:T(128)S(1)} %get-tuple-element.693, f32[1024]{0:T(1024)S(1)} %bitcast.239, f32[128]{0:T(128)S(1)} %get-tuple-element.695, ...), kind=kLoop, calls=%fused_computation.129.clone.1 | loop fusion | flops 3670016 | bytes 2635268 | tf_op jit(solution)/shard_map/convert.4
  107.8 3.2 %fusion.207 = (bf16[128,1024]{1,0:T(8,128)(2,1)S(1)}, bf16[128,1024]{1,0:T(8,128)(2,1)S(1)}, f32[128,1024]{1,0:T(8,128)S(1)}, f32[128,1024]{1,0:T(8,128)S(1)}) fusion(f32[1024]{0:T(1024)S(1)} %bitcast.237, f32[128]{0:T(128)S(1)} %get-tuple-element.693, f32[1024]{0:T(1024)S(1)} %bitcast.239, f32[128]{0:T(128)S(1)} %get-tuple-element.695, ...), kind=kLoop, calls=%fused_computation.129.clone.1 | loop fusion | flops 3670016 | bytes 2635268 | tf_op jit(solution)/shard_map/convert.4
  112.2 3.2 %fusion.207 = (bf16[128,1024]{1,0:T(8,128)(2,1)S(1)}, bf16[128,1024]{1,0:T(8,128)(2,1)S(1)}, f32[128,1024]{1,0:T(8,128)S(1)}, f32[128,1024]{1,0:T(8,128)S(1)}) fusion(f32[1024]{0:T(1024)S(1)} %bitcast.237, f32[128]{0:T(128)S(1)} %get-tuple-element.693, f32[1024]{0:T(1024)S(1)} %bitcast.239, f32[128]{0:T(128)S(1)} %get-tuple-element.695, ...), kind=kLoop, calls=%fused_computation.129.clone.1 | loop fusion | flops 3670016 | bytes 2635268 | tf_op jit(solution)/shard_map/convert.4
  116.5 3.2 %fusion.207 = (bf16[128,1024]{1,0:T(8,128)(2,1)S(1)}, bf16[128,1024]{1,0:T(8,128)(2,1)S(1)}, f32[128,1024]{1,0:T(8,128)S(1)}, f32[128,1024]{1,0:T(8,128)S(1)}) fusion(f32[1024]{0:T(1024)S(1)} %bitcast.237, f32[128]{0:T(128)S(1)} %get-tuple-element.693, f32[1024]{0:T(1024)S(1)} %bitcast.239, f32[128]{0:T(128)S(1)} %get-tuple-element.695, ...), kind=kLoop, calls=%fused_computation.129.clone.1 | loop fusion | flops 3670016 | bytes 2635268 | tf_op jit(solution)/shard_map/convert.4
  120.8 3.2 %fusion.207 = (bf16[128,1024]{1,0:T(8,128)(2,1)S(1)}, bf16[128,1024]{1,0:T(8,128)(2,1)S(1)}, f32[128,1024]{1,0:T(8,128)S(1)}, f32[128,1024]{1,0:T(8,128)S(1)}) fusion(f32[1024]{0:T(1024)S(1)} %bitcast.237, f32[128]{0:T(128)S(1)} %get-tuple-element.693, f32[1024]{0:T(1024)S(1)} %bitcast.239, f32[128]{0:T(128)S(1)} %get-tuple-element.695, ...), kind=kLoop, calls=%fused_computation.129.clone.1 | loop fusion | flops 3670016 | bytes 2635268 | tf_op jit(solution)/shard_map/convert.4
  125.1 3.2 %fusion.207 = (bf16[128,1024]{1,0:T(8,128)(2,1)S(1)}, bf16[128,1024]{1,0:T(8,128)(2,1)S(1)}, f32[128,1024]{1,0:T(8,128)S(1)}, f32[128,1024]{1,0:T(8,128)S(1)}) fusion(f32[1024]{0:T(1024)S(1)} %bitcast.237, f32[128]{0:T(128)S(1)} %get-tuple-element.693, f32[1024]{0:T(1024)S(1)} %bitcast.239, f32[128]{0:T(128)S(1)} %get-tuple-element.695, ...), kind=kLoop, calls=%fused_computation.129.clone.1 | loop fusion | flops 3670016 | bytes 2635268 | tf_op jit(solution)/shard_map/convert.4
  130.9 13.6 %all-gather = f32[8,32,32]{2,1,0:T(8,128)S(1)} all-gather(f32[2,32,32]{2,1,0:T(8,128)S(1)} %copy.12), channel_id=2, replica_groups=mesh['case'=2,'blk'=4,'freq'=4] {'blk'}, dimensions={0}, use_global_device_ids=true | all-gather | bytes 40960 | tf_op jit(solution)/shard_map/all_gather | solution.py:139
  146.4 20.6 %reduce-scatter.4.cloned.1.call-done = f32[256,3]{1,0:T(8,128)} async-done(((f32[1024,3]{1,0:T(8,128)}), f32[256,3]{1,0:T(8,128)}) %reduce-scatter.4.cloned.1.call-update) | async-done | bytes 3088
  (251 shorter events, 40.5 us)
Async XLA Ops:
  7.2 159.8 %reduce-scatter.4.cloned.1.call-start = ((), (), s32[]{:S(2)}) async-start(), calls=%async_computation.1 | async-start | bytes 655360
  7.2 46.3 %collective-permute-start.1 = (bf16[1024,128]{1,0:T(8,128)(2,1)}, bf16[1024,128]{1,0:T(8,128)(2,1)S(1)}, u32[]{:S(2)}, u32[]{:S(2)}) collective-permute-start(bf16[1024,128]{1,0:T(8,128)(2,1)} %bitcast.220), channel_id=1, source_target_pairs={{0,4},{4,8},{8,12},{12,0},{1,5},{5,9},{9,13},{13,1},{2,6},{6,10},{... | collective-permute-start | bytes 786440 | tf_op jit(solution)/shard_map/ppermute | solution.py:14
  10.3 8.7 %collective-permute-start = (bf16[3,1024]{1,0:T(4,128)(2,1)}, bf16[3,1024]{1,0:T(4,128)(2,1)S(1)}, u32[]{:S(2)}, u32[]{:S(2)}) collective-permute-start(bf16[3,1024]{1,0:T(4,128)(2,1)} %param.10), channel_id=1, source_target_pairs={{0,4},{4,8},{8,12},{12,0},{1,5},{5,9},{9,13},{13,1},{2,6},{6,10},{... | collective-permute-start | bytes 18440 | tf_op jit(solution)/shard_map/ppermute | solution.py:14
  11.9 1.7 copy-start
  13.7 0.7 copy-start.2
  13.7 0.7 copy-start.3
  14.8 1.2 copy-start.1
  19.0 34.5 %collective-permute-start.2 = (bf16[3,1024]{1,0:T(4,128)(2,1)S(1)}, bf16[3,1024]{1,0:T(4,128)(2,1)S(1)}, u32[]{:S(2)}, u32[]{:S(2)}) collective-permute-start(bf16[3,1024]{1,0:T(4,128)(2,1)S(1)} %collective-permute-done), channel_id=1, source_target_pairs={{0,4},{4,8},{8,12},{12,0},{1,5},{5,9},{9,13},{13,1},{2,6},{6,10},{... | collective-permute-start | bytes 18440 | tf_op jit(solution)/shard_map/ppermute | solution.py:14
  54.7 38.7 %collective-permute-start.3 = (bf16[1024,128]{1,0:T(8,128)(2,1)S(1)}, bf16[1024,128]{1,0:T(8,128)(2,1)S(1)}, u32[]{:S(2)}, u32[]{:S(2)}) collective-permute-start(bf16[1024,128]{1,0:T(8,128)(2,1)S(1)} %collective-permute-done.1), channel_id=1, source_target_pairs={{0,4},{4,8},{8,12},{12,0},{1,5},{5,9},{9,13},{13,1},{2,6},{6,10},{... | collective-permute-start | bytes 786440 | tf_op jit(solution)/shard_map/ppermute | solution.py:14
  90.8 53.8 %collective-permute-start.4 = (f32[3,1024]{1,0:T(4,128)S(1)}, f32[3,1024]{1,0:T(4,128)S(1)}, u32[]{:S(2)}, u32[]{:S(2)}) collective-permute-start(f32[3,1024]{1,0:T(4,128)S(1)} %get-tuple-element.168), channel_id=1, source_target_pairs={{0,12},{4,0},{8,4},{12,8},{1,13},{5,1},{9,5},{13,9},{2,14},{6,2},{... | collective-permute-start | bytes 36872 | tf_op jit(solution)/shard_map/ppermute | solution.py:14
  130.3 14.3 %collective-permute-start.5 = (f32[3,1024]{1,0:T(4,128)S(1)}, f32[3,1024]{1,0:T(4,128)S(1)}, u32[]{:S(2)}, u32[]{:S(2)}) collective-permute-start(f32[3,1024]{1,0:T(4,128)S(1)} %get-tuple-element.169), channel_id=1, source_target_pairs={{0,8},{4,12},{8,0},{12,4},{1,9},{5,13},{9,1},{13,5},{2,10},{6,14},... | collective-permute-start | bytes 36872 | tf_op jit(solution)/shard_map/ppermute | solution.py:14
Sparse Core Ops, SparseCore 0:
  145.8 21.1 reduce-scatter.3
